TPU v7x, 256 devices: a whole 4x4x8 slice. The times are simulated.
256 devices in a mesh: col: 64 (over y, z, core), row: 4 (over x).
Axes of the slice: x: 4, y: 4, z: 8, core: 2. Of those that a mesh axis runs over, the one named last changes fastest.
Arguments:
- r_slab: float32 [1024, 16384], P('row', 'col'), may hold values from -4 to 8, as said below
- arc_rows: float32 [4096, 16384], P('row', 'col'), may hold values from -6 to 6
- arc_blocks: int32 [32, 64], P('row', 'col'), may hold values 0 or 1
Outputs:
- r_updated: float32 [1024, 16384], P('row', 'col')
Inputs may be any that keep to these rules, and one draw needn't show every extreme that they name: r_slab is zero wherever an entry's global column index is below its row index, and its diagonal is positive.
All inputs are finite; a program needn't handle non-finite values. No bound on the sum of `arc_blocks` on one device may be relied on, other than what follows from the above.
Results may differ from a plain program's by a relative error of at most 0.000098.
Values sent between devices are 32-bit elements; how exact they have to be, the bound alone decides.
A program may use at most 64 MiB of HBM per device.

v0:
```python
import jax
import jax.numpy as jnp
from jax import lax
from jax.sharding import PartitionSpec as P

B = 256
P_SIZE = 4
ARC_ROWS = 128
HI = lax.Precision.HIGHEST


def inner_dot(left, right):
    return lax.dot_general(left, right, (((0,), (0,)), ((), ())), precision=HI)


def plain_dot(left, right):
    return jnp.dot(left, right, precision=HI)


def on_device(r_slab, arc_rows, arc_blocks):
    n_col = lax.axis_size("col")
    col_index = lax.axis_index("col")
    row_index = lax.axis_index("row")
    n_arcs, blocks_here = arc_blocks.shape
    lead = P_SIZE * B
    live = arc_blocks.astype(jnp.float32)
    masked = (arc_rows.reshape(n_arcs, ARC_ROWS, blocks_here, B) * live[:, None, :, None]).reshape(
        arc_rows.shape
    )
    stacked = jnp.concatenate([r_slab, masked], axis=0)
    height = stacked.shape[0]
    part = height // n_col
    pieces = stacked.reshape(n_col, part, B)
    pieces = lax.all_to_all(pieces, "col", split_axis=0, concat_axis=0, tiled=True)
    mine = pieces[:P_SIZE]
    panels = lax.all_gather(mine, "col")
    panels = panels.transpose(0, 2, 1, 3).reshape(height, lead)
    share = lead // n_col
    own = lax.dynamic_slice(panels, (0, col_index * share), (height, share))
    gram_part = lax.psum(inner_dot(own, panels), "row")
    gram = lax.all_gather(gram_part, "col", tiled=True)
    rhs = lax.psum(inner_dot(panels, stacked), "row")
    lower = jnp.linalg.cholesky(gram, symmetrize_input=False)
    factor = jax.scipy.linalg.solve_triangular(lower, rhs, lower=True)
    mine_out = lax.dynamic_slice(factor, (row_index * B, 0), (B, B))
    row_ids = row_index * B + lax.broadcasted_iota(jnp.int32, (B, B), 0)
    col_ids = col_index * B + lax.broadcasted_iota(jnp.int32, (B, B), 1)
    return jnp.where(col_ids >= row_ids, mine_out, jnp.zeros_like(mine_out))


def solution(mesh):
    return jax.shard_map(
        on_device,
        mesh=mesh,
        in_specs=(P("row", "col"), P("row", "col"), P("row", "col")),
        out_specs=P("row", "col"),
        check_vma=False,
    )
```

profile of v0, /device:TPU:1, one launch (start us, length us, event | category | flops | bytes accessed | tf_op | source)
XLA Modules:
  0.0 636.5 jit_solution(12063077370027670616)
XLA Ops:
  12.2 52.7 %all_to_all.5 = f32[64,20,256]{2,1,0:T(8,128)S(1)} all-to-all(f32[64,20,256]{2,1,0:T(8,128)S(1)} %reshape.90), channel_id=1, replica_groups=mesh['col'=64,'row'=4] {'col'}, dimensions={0} | all-to-all | bytes 2621440 | tf_op jit(solution)/shard_map/all_to_all | solution.py:34
  65.7 78.4 %all-gather.6.cloned.1.call-done = f32[256,20,256]{2,1,0:T(8,128)} async-done(((f32[4,20,256]{2,1,0:T(8,128)}), f32[256,20,256]{2,1,0:T(8,128)}) %all-gather.6.cloned.1.call-update) | async-done | bytes 5242896 | tf_op jit(solution)/shard_map/all_gather | solution.py:36
  144.1 5.2 copy.5
  150.5 9.5 %fusion.63 = f32[1024,256]{1,0:T(8,128)} fusion(f32[1280,1024]{1,0:T(8,128)S(1)} %bitcast.108, f32[1024,256]{1,0:T(8,128)S(1)} %broadcast_multiply_fusion, f32[256,256]{1,0:T(8,128)S(1)} %copy-done), kind=kOutput, calls=%fused_computation.162 | convolution fusion | flops 4026859520 | bytes 7602176 | tf_op jit(solution)/shard_map/dot_general | solution.py:13
  160.1 14.3 %fusion.5 = f32[16,1024]{1,0:T(8,128)} fusion(f32[1280,1024]{1,0:T(8,128)S(1)} %bitcast.109, s32[]{:T(128)S(6)} %select_n.14), kind=kOutput, calls=%fused_computation.31 | convolution fusion | flops 251658240 | bytes 5963780 | tf_op jit(solution)/shard_map/dot_general | solution.py:13
  174.4 46.4 %all-reduce.4.cloned.1.call-done = (f32[1024,256]{1,0:T(8,128)}, f32[16,1024]{1,0:T(8,128)}) async-done(((f32[1024,256]{1,0:T(8,128)}, f32[16,1024]{1,0:T(8,128)}), (f32[1024,256]{1,0:T(8,128)}, f32[16,1024]{1,0:T(8,128)})) %all-reduce.4.cloned.1.call-update) | async-done | bytes 1114128 | tf_op jit(solution)/shard_map/psum | solution.py:42
  220.8 84.7 %all-gather.4.cloned.1.call-done = f32[1024,1024]{1,0:T(8,128)} async-done(((f32[16,1024]{1,0:T(8,128)}), f32[1024,1024]{1,0:T(8,128)}) %all-gather.4.cloned.1.call-update) | async-done | bytes 4194320 | tf_op jit(solution)/shard_map/all_gather | solution.py:41
  306.4 11.7 %cholesky.223 = f32[128,128]{1,0:T(8,128)S(1)} custom-call(f32[128,128]{1,0:T(8,128)S(1)} %cholesky.580), custom_call_target="Cholesky" | custom-call | tf_op jit(solution)/shard_map/jit(cholesky)/cholesky | solution.py:43
  318.1 9.8 %custom-call.63 = f32[1,128,128]{1,2,0:T(8,128)S(1)} custom-call(f32[1,128,128]{2,1,0:T(8,128)S(1)} %get-tuple-element.71), custom_call_target="InvertDiagBlocksLowerTriangular" | custom-call | tf_op jit(solution)/shard_map/jit(cholesky)/cholesky | solution.py:43
  328.0 2.5 cholesky.255
  330.5 2.4 constant_dynamic-update-slice_fusion.31
  334.4 11.7 %cholesky.244 = f32[128,128]{1,0:T(8,128)S(1)} custom-call(f32[128,128]{1,0:T(8,128)S(1)} %cholesky.584), custom_call_target="Cholesky" | custom-call | tf_op jit(solution)/shard_map/jit(cholesky)/cholesky | solution.py:43
  346.8 10.2 %custom-call.64 = f32[1,128,128]{1,2,0:T(8,128)S(1)} custom-call(f32[1,128,128]{2,1,0:T(8,128)S(1)} %get-tuple-element.68), custom_call_target="InvertDiagBlocksLowerTriangular" | custom-call | tf_op jit(solution)/shard_map/jit(cholesky)/cholesky | solution.py:43
  360.3 11.7 %cholesky.468 = f32[128,128]{1,0:T(8,128)S(1)} custom-call(f32[128,128]{1,0:T(8,128)S(1)} %cholesky.589), custom_call_target="Cholesky" | custom-call | tf_op jit(solution)/shard_map/jit(cholesky)/cholesky | solution.py:43
  373.4 9.8 %custom-call.65 = f32[1,128,128]{1,2,0:T(8,128)S(1)} custom-call(f32[1,128,128]{2,1,0:T(8,128)S(1)} %get-tuple-element.65), custom_call_target="InvertDiagBlocksLowerTriangular" | custom-call | tf_op jit(solution)/shard_map/jit(cholesky)/cholesky | solution.py:43
  384.3 2.3 convolution_subtract_fusion.2
  386.7 11.9 %cholesky.487 = f32[128,128]{1,0:T(8,128)S(1)} custom-call(f32[128,128]{1,0:T(8,128)S(1)} %cholesky.594), custom_call_target="Cholesky" | custom-call | tf_op jit(solution)/shard_map/jit(cholesky)/cholesky | solution.py:43
  399.9 9.8 %custom-call.66 = f32[1,128,128]{1,2,0:T(8,128)S(1)} custom-call(f32[1,128,128]{2,1,0:T(8,128)S(1)} %get-tuple-element.62), custom_call_target="InvertDiagBlocksLowerTriangular" | custom-call | tf_op jit(solution)/shard_map/jit(cholesky)/cholesky | solution.py:43
  410.8 2.3 convolution_subtract_fusion.3
  413.2 11.7 %cholesky.506 = f32[128,128]{1,0:T(8,128)S(1)} custom-call(f32[128,128]{1,0:T(8,128)S(1)} %cholesky.599), custom_call_target="Cholesky" | custom-call | tf_op jit(solution)/shard_map/jit(cholesky)/cholesky | solution.py:43
  426.2 9.8 %custom-call.67 = f32[1,128,128]{1,2,0:T(8,128)S(1)} custom-call(f32[1,128,128]{2,1,0:T(8,128)S(1)} %get-tuple-element.59), custom_call_target="InvertDiagBlocksLowerTriangular" | custom-call | tf_op jit(solution)/shard_map/jit(cholesky)/cholesky | solution.py:43
  437.1 2.5 convolution_subtract_fusion.4
  439.6 11.7 %cholesky.526 = f32[128,128]{1,0:T(8,128)S(1)} custom-call(f32[128,128]{1,0:T(8,128)S(1)} %cholesky.604), custom_call_target="Cholesky" | custom-call | tf_op jit(solution)/shard_map/jit(cholesky)/cholesky | solution.py:43
  452.7 9.8 %custom-call.68 = f32[1,128,128]{1,2,0:T(8,128)S(1)} custom-call(f32[1,128,128]{2,1,0:T(8,128)S(1)} %get-tuple-element.56), custom_call_target="InvertDiagBlocksLowerTriangular" | custom-call | tf_op jit(solution)/shard_map/jit(cholesky)/cholesky | solution.py:43
  465.5 11.7 %cholesky.546 = f32[128,128]{1,0:T(8,128)S(1)} custom-call(f32[128,128]{1,0:T(8,128)S(1)} %cholesky.609), custom_call_target="Cholesky" | custom-call | tf_op jit(solution)/shard_map/jit(cholesky)/cholesky | solution.py:43
  478.5 10.2 %custom-call.69 = f32[1,128,128]{1,2,0:T(8,128)S(1)} custom-call(f32[1,128,128]{2,1,0:T(8,128)S(1)} %get-tuple-element.53), custom_call_target="InvertDiagBlocksLowerTriangular" | custom-call | tf_op jit(solution)/shard_map/jit(cholesky)/cholesky | solution.py:43
  491.3 11.7 %cholesky.564 = f32[128,128]{1,0:T(8,128)S(1)} custom-call(f32[128,128]{1,0:T(8,128)S(1)} %convolution_subtract_fusion.13), custom_call_target="Cholesky" | custom-call | tf_op jit(solution)/shard_map/jit(cholesky)/cholesky | solution.py:43
  510.1 4.9 select_select_fusion
  515.0 23.1 %while.1 = (s32[]{:T(128)}, f32[1024,1024]{1,0:T(8,128)}, s32[8,2]{0,1:T(2,128)S(1)}, f32[8,128,128]{2,1,0:T(8,128)S(1)}, s32[]{:T(128)}) while((s32[]{:T(128)}, f32[1024,1024]{1,0:T(8,128)}, s32[8,2]{0,1:T(2,128)S(1)}, f32[8,128,128]{2,1,0:T(8,128)S(1)}, s32[]{:T(128)}) %tuple.58), condition=%wide.while_cond, body=%wide.while_body.sunk | while | flops 2 | bytes 131181 | solution.py:44
  515.7 2.3 bitcast_dynamic-update-slice_fusion.2
  518.6 2.3 bitcast_dynamic-update-slice_fusion.2
  538.1 78.6 %custom-call.70 = f32[8,128,128]{1,2,0:T(8,128)S(1)} custom-call(f32[8,128,128]{2,1,0:T(8,128)S(1)} %get-tuple-element.12), custom_call_target="InvertDiagBlocksLowerTriangular" | custom-call | tf_op jit(solution)/shard_map/jit(_solve_triangular)/triangular_solve | solution.py:44
  (91 shorter events, 62.9 us)
Async XLA Ops:
  6.5 137.5 %all-gather.6.cloned.1.call-start = ((), (), s32[]{:S(2)}) async-start(), calls=%async_computation.2 | async-start | bytes 6389760 | tf_op jit(solution)/shard_map/all_gather | solution.py:36
  65.6 155.2 %all-reduce.4.cloned.1.call-start = ((), (), s32[]{:S(2)}) async-start(), calls=%async_computation.3 | async-start | bytes 2228224 | tf_op jit(solution)/shard_map/psum | solution.py:42
  149.2 1.3 copy-start
  174.4 131.2 %all-gather.4.cloned.1.call-start = ((), (), s32[]{:S(2)}) async-start(), calls=%async_computation.1 | async-start | bytes 4259840 | tf_op jit(solution)/shard_map/all_gather | solution.py:41
  510.1 106.6 %copy-start.1 = (f32[1024,256]{1,0:T(8,128)S(1)}, f32[1024,256]{1,0:T(8,128)}, u32[]{:S(2)}) copy-start(f32[1024,256]{1,0:T(8,128)} %get-tuple-element.21) | copy-start | bytes 3145732
Sparse Core Ops, SparseCore 0:
  65.7 78.2 all-gather.5
  174.5 46.2 all-reduce.3
  223.9 81.5 all-gather.3
where the time goes:
time: 647 us; the launch traced here: 636 us
  other arithmetic  261 us (40%)
  waiting for transfers between devices  210 us (32%)
  matrix products  59.2 us (9%)
  blocking collectives  52.7 us (8%)
  local copies, waits for them, and re-layouts  34.8 us (5%)
  between operations  18.8 us (3%)
    another operation x30, other arithmetic, on_device(): lower = jnp.linalg.cholesky(gram, symmetrize_input=False)  173 us
    all_gather x1, waiting for transfers between devices, on_device(): gram = lax.all_gather(gram_part, 'col', tiled=True)  84.7 us
    another operation x3, other arithmetic, on_device(): factor = jax.scipy.linalg.solve_triangular(lower, rhs, lower=True)  83.5 us
    all_gather x1, waiting for transfers between devices, on_device(): panels = lax.all_gather(mine, 'col')  78.4 us
    all_to_all x1, blocking collectives, on_device(): lax.all_to_all(pieces, 'col', split_axis=0, concat_axis=0, tiled=True)  52.7 us
    psum x1, waiting for transfers between devices, on_device(): rhs = lax.psum(inner_dot(panels, stacked), 'row')  46.4 us
    dot_general x2, matrix products, inner_dot(): return lax.dot_general(left, right, (((0,), (0,)), ((), ())), precision=HI)  23.8 us
    another operation x14, matrix products, on_device(): lower = jnp.linalg.cholesky(gram, symmetrize_input=False)  23.3 us
  transfers between devices with their start and end apart: 3, of which 3 were waited for; matrix products, arithmetic and copies ran while one was open for 0% of the time, Pallas kernels for 0%

commit v1 on v0

--- a/solution.py
+++ b/solution.py
@@ -39,7 +39,7 @@
     own = lax.dynamic_slice(panels, (0, col_index * share), (height, share))
     gram_part = lax.psum(inner_dot(own, panels), "row")
     gram = lax.all_gather(gram_part, "col", tiled=True)
-    rhs = lax.psum(inner_dot(panels, stacked), "row")
+    rhs = jnp.sum(lax.all_gather(inner_dot(panels, stacked), "row"), axis=0)
     lower = jnp.linalg.cholesky(gram, symmetrize_input=False)
     factor = jax.scipy.linalg.solve_triangular(lower, rhs, lower=True)
     mine_out = lax.dynamic_slice(factor, (row_index * B, 0), (B, B))

time: 647 us -> 673 us (1.040)
  waiting for transfers between devices: 210 us -> 241 us
  matrix products: 59.2 us -> 50.8 us
    all_gather x0 -> x1, waiting for transfers between devices: none -> 55.2 us  [on_device(): rhs = jnp.sum(lax.all_gather(inner_dot(panels, stacked), 'row'), axis=0)]
    psum x1, waiting for transfers between devices: 46.4 us -> 27.5 us  [on_device(): gram_part = lax.psum(inner_dot(own, panels), 'row')]
    dot_general x2, matrix products: 23.8 us -> 15.4 us  [inner_dot(): return lax.dot_general(left, right, (((0,), (0,)), ((), ())), precision=HI)]
  transfers between devices with their start and end apart: 3 -> 4, of which waited for: 3 -> 4; matrix products, arithmetic and copies ran while one was open for 0% -> 2% of each run, Pallas kernels for 0% -> 0%
where the time goes in v1:
time: 673 us; the launch traced here: 665 us
  other arithmetic  263 us (39%)
  waiting for transfers between devices  241 us (36%)
  blocking collectives  52.7 us (8%)
  matrix products  50.8 us (8%)
  local copies, waits for them, and re-layouts  37.1 us (6%)
  between operations  18.7 us (3%)
    another operation x30, other arithmetic, on_device(): lower = jnp.linalg.cholesky(gram, symmetrize_input=False)  172 us
    another operation x3, other arithmetic, on_device(): factor = jax.scipy.linalg.solve_triangular(lower, rhs, lower=True)  83.4 us
    all_gather x1, waiting for transfers between devices, on_device(): gram = lax.all_gather(gram_part, 'col', tiled=True)  80.4 us
    all_gather x1, waiting for transfers between devices, on_device(): panels = lax.all_gather(mine, 'col')  78.4 us
    all_gather x1, waiting for transfers between devices, on_device(): rhs = jnp.sum(lax.all_gather(inner_dot(panels, stacked), 'row'), axis=0)  55.2 us
    all_to_all x1, blocking collectives, on_device(): lax.all_to_all(pieces, 'col', split_axis=0, concat_axis=0, tiled=True)  52.7 us
    psum x1, waiting for transfers between devices, on_device(): gram_part = lax.psum(inner_dot(own, panels), 'row')  27.5 us
    another operation x14, matrix products, on_device(): lower = jnp.linalg.cholesky(gram, symmetrize_input=False)  23.3 us
  transfers between devices with their start and end apart: 4, of which 4 were waited for; matrix products, arithmetic and copies ran while one was open for 2% of the time, Pallas kernels for 0%

profile of v1, /device:TPU:1, one launch (start us, length us, event | category | flops | bytes accessed | tf_op | source)
XLA Modules:
  0.0 665.1 jit_solution(9641180798195656786)
XLA Ops:
  12.2 52.7 %all_to_all.5 = f32[64,20,256]{2,1,0:T(8,128)S(1)} all-to-all(f32[64,20,256]{2,1,0:T(8,128)S(1)} %reshape.90), channel_id=1, replica_groups=mesh['col'=64,'row'=4] {'col'}, dimensions={0} | all-to-all | bytes 2621440 | tf_op jit(solution)/shard_map/all_to_all | solution.py:34
  65.7 78.4 %all-gather.8.cloned.1.call-done = f32[256,20,256]{2,1,0:T(8,128)} async-done(((f32[4,20,256]{2,1,0:T(8,128)}), f32[256,20,256]{2,1,0:T(8,128)}) %all-gather.8.cloned.1.call-update) | async-done | bytes 5242896 | tf_op jit(solution)/shard_map/all_gather | solution.py:36
  144.1 5.2 copy.5
  152.8 3.6 fusion.5
  157.0 11.8 %fusion.63 = f32[1024,256]{1,0:T(8,128)} fusion(f32[1280,1024]{1,0:T(8,128)} %bitcast.110, f32[1024,256]{1,0:T(8,128)S(1)} %broadcast_multiply_fusion, f32[256,256]{1,0:T(8,128)S(1)} %copy-done.1), kind=kOutput, calls=%fused_computation.162 | convolution fusion | flops 4026859520 | bytes 7602176 | tf_op jit(solution)/shard_map/dot_general | solution.py:13
  169.1 27.5 %all-reduce.3.cloned.1.call-done = f32[16,1024]{1,0:T(8,128)} async-done(((f32[16,1024]{1,0:T(8,128)}), f32[16,1024]{1,0:T(8,128)}) %all-reduce.3.cloned.1.call-update) | async-done | bytes 65552 | tf_op jit(solution)/shard_map/psum | solution.py:40
  196.7 55.2 %all-gather.10.cloned.1.call-done = f32[4096,256]{1,0:T(8,128)} async-done(((f32[1024,256]{1,0:T(8,128)}), f32[4096,256]{1,0:T(8,128)}) %all-gather.10.cloned.1.call-update) | async-done | bytes 4194320 | tf_op jit(solution)/shard_map/all_gather | solution.py:42
  251.9 2.6 reduce_sum.9
  254.5 80.4 %all-gather.6.cloned.1.call-done = f32[1024,1024]{1,0:T(8,128)} async-done(((f32[16,1024]{1,0:T(8,128)}), f32[1024,1024]{1,0:T(8,128)}) %all-gather.6.cloned.1.call-update) | async-done | bytes 4194320 | tf_op jit(solution)/shard_map/all_gather | solution.py:41
  335.7 11.7 %cholesky.223 = f32[128,128]{1,0:T(8,128)S(1)} custom-call(f32[128,128]{1,0:T(8,128)S(1)} %cholesky.580), custom_call_target="Cholesky" | custom-call | tf_op jit(solution)/shard_map/jit(cholesky)/cholesky | solution.py:43
  347.4 2.5 cholesky.255
  349.9 9.8 %custom-call.63 = f32[1,128,128]{1,2,0:T(8,128)S(1)} custom-call(f32[1,128,128]{2,1,0:T(8,128)S(1)} %get-tuple-element.69), custom_call_target="InvertDiagBlocksLowerTriangular" | custom-call | tf_op jit(solution)/shard_map/jit(cholesky)/cholesky | solution.py:43
  359.7 2.4 constant_dynamic-update-slice_fusion.31
  363.7 11.7 %cholesky.244 = f32[128,128]{1,0:T(8,128)S(1)} custom-call(f32[128,128]{1,0:T(8,128)S(1)} %cholesky.584), custom_call_target="Cholesky" | custom-call | tf_op jit(solution)/shard_map/jit(cholesky)/cholesky | solution.py:43
  376.0 10.0 %custom-call.64 = f32[1,128,128]{1,2,0:T(8,128)S(1)} custom-call(f32[1,128,128]{2,1,0:T(8,128)S(1)} %get-tuple-element.66), custom_call_target="InvertDiagBlocksLowerTriangular" | custom-call | tf_op jit(solution)/shard_map/jit(cholesky)/cholesky | solution.py:43
  389.4 11.7 %cholesky.468 = f32[128,128]{1,0:T(8,128)S(1)} custom-call(f32[128,128]{1,0:T(8,128)S(1)} %cholesky.589), custom_call_target="Cholesky" | custom-call | tf_op jit(solution)/shard_map/jit(cholesky)/cholesky | solution.py:43
  401.7 9.8 %custom-call.65 = f32[1,128,128]{1,2,0:T(8,128)S(1)} custom-call(f32[1,128,128]{2,1,0:T(8,128)S(1)} %get-tuple-element.63), custom_call_target="InvertDiagBlocksLowerTriangular" | custom-call | tf_op jit(solution)/shard_map/jit(cholesky)/cholesky | solution.py:43
  412.7 2.3 convolution_subtract_fusion.2
  415.0 12.1 %cholesky.487 = f32[128,128]{1,0:T(8,128)S(1)} custom-call(f32[128,128]{1,0:T(8,128)S(1)} %cholesky.594), custom_call_target="Cholesky" | custom-call | tf_op jit(solution)/shard_map/jit(cholesky)/cholesky | solution.py:43
  427.8 9.8 %custom-call.66 = f32[1,128,128]{1,2,0:T(8,128)S(1)} custom-call(f32[1,128,128]{2,1,0:T(8,128)S(1)} %get-tuple-element.60), custom_call_target="InvertDiagBlocksLowerTriangular" | custom-call | tf_op jit(solution)/shard_map/jit(cholesky)/cholesky | solution.py:43
  438.7 2.3 convolution_subtract_fusion.3
  441.1 11.7 %cholesky.506 = f32[128,128]{1,0:T(8,128)S(1)} custom-call(f32[128,128]{1,0:T(8,128)S(1)} %cholesky.599), custom_call_target="Cholesky" | custom-call | tf_op jit(solution)/shard_map/jit(cholesky)/cholesky | solution.py:43
  453.4 9.8 %custom-call.67 = f32[1,128,128]{1,2,0:T(8,128)S(1)} custom-call(f32[1,128,128]{2,1,0:T(8,128)S(1)} %get-tuple-element.57), custom_call_target="InvertDiagBlocksLowerTriangular" | custom-call | tf_op jit(solution)/shard_map/jit(cholesky)/cholesky | solution.py:43
  464.3 2.5 convolution_subtract_fusion.4
  466.8 11.7 %cholesky.526 = f32[128,128]{1,0:T(8,128)S(1)} custom-call(f32[128,128]{1,0:T(8,128)S(1)} %cholesky.604), custom_call_target="Cholesky" | custom-call | tf_op jit(solution)/shard_map/jit(cholesky)/cholesky | solution.py:43
  479.1 9.8 %custom-call.68 = f32[1,128,128]{1,2,0:T(8,128)S(1)} custom-call(f32[1,128,128]{2,1,0:T(8,128)S(1)} %get-tuple-element.54), custom_call_target="InvertDiagBlocksLowerTriangular" | custom-call | tf_op jit(solution)/shard_map/jit(cholesky)/cholesky | solution.py:43
  491.9 11.7 %cholesky.546 = f32[128,128]{1,0:T(8,128)S(1)} custom-call(f32[128,128]{1,0:T(8,128)S(1)} %cholesky.609), custom_call_target="Cholesky" | custom-call | tf_op jit(solution)/shard_map/jit(cholesky)/cholesky | solution.py:43
  504.3 10.0 %custom-call.69 = f32[1,128,128]{1,2,0:T(8,128)S(1)} custom-call(f32[1,128,128]{2,1,0:T(8,128)S(1)} %get-tuple-element.51), custom_call_target="InvertDiagBlocksLowerTriangular" | custom-call | tf_op jit(solution)/shard_map/jit(cholesky)/cholesky | solution.py:43
  516.9 11.7 %cholesky.564 = f32[128,128]{1,0:T(8,128)S(1)} custom-call(f32[128,128]{1,0:T(8,128)S(1)} %convolution_subtract_fusion.13), custom_call_target="Cholesky" | custom-call | tf_op jit(solution)/shard_map/jit(cholesky)/cholesky | solution.py:43
  538.6 4.8 select_select_fusion
  543.4 23.2 %while.1 = (s32[]{:T(128)}, f32[1024,1024]{1,0:T(8,128)}, s32[8,2]{0,1:T(2,128)S(1)}, f32[8,128,128]{2,1,0:T(8,128)S(1)}, s32[]{:T(128)}) while((s32[]{:T(128)}, f32[1024,1024]{1,0:T(8,128)}, s32[8,2]{0,1:T(2,128)S(1)}, f32[8,128,128]{2,1,0:T(8,128)S(1)}, s32[]{:T(128)}) %tuple.57), condition=%wide.while_cond, body=%wide.while_body.sunk | while | flops 2 | bytes 131189 | solution.py:44
  566.6 78.6 %custom-call.70 = f32[8,128,128]{1,2,0:T(8,128)S(1)} custom-call(f32[8,128,128]{2,1,0:T(8,128)S(1)} %get-tuple-element.12), custom_call_target="InvertDiagBlocksLowerTriangular" | custom-call | tf_op jit(solution)/shard_map/jit(_solve_triangular)/triangular_solve | solution.py:44
  (96 shorter events, 70.2 us)
Async XLA Ops:
  6.5 137.5 %all-gather.8.cloned.1.call-start = ((), (), s32[]{:S(2)}) async-start(), calls=%async_computation.3 | async-start | bytes 6389760 | tf_op jit(solution)/shard_map/all_gather | solution.py:36
  65.6 131.0 %all-reduce.3.cloned.1.call-start = ((), (), s32[]{:S(2)}) async-start(), calls=%async_computation.1 | async-start | bytes 131072 | tf_op jit(solution)/shard_map/psum | solution.py:40
  150.5 2.3 copy-start
  150.5 6.5 copy-start.1
  156.4 95.4 %all-gather.10.cloned.1.call-start = ((), (), s32[]{:S(2)}) async-start(), calls=%async_computation.4 | async-start | bytes 5242880 | tf_op jit(solution)/shard_map/all_gather | solution.py:42
  168.9 165.9 %all-gather.6.cloned.1.call-start = ((), (), s32[]{:S(2)}) async-start(), calls=%async_computation.2 | async-start | bytes 4259840 | tf_op jit(solution)/shard_map/all_gather | solution.py:41
Sparse Core Ops, SparseCore 0:
  65.7 78.2 all-gather.7
  156.5 40.0 all-reduce.2
  198.6 53.2 all-gather.9
  254.9 79.8 all-gather.5
